TPU v7x, 32 devices: a whole 2x2x4 slice. The times are simulated.
32 devices in a mesh: row: 8 (over z, x), col: 4 (over y, core).
Axes of the slice: x: 2, y: 2, z: 4, core: 2. Of those that a mesh axis runs over, the one named last changes fastest.
Arguments:
- diag_inverse: bfloat16 [2, 8192, 8192], P(None, 'col', 'row'), as said below
- panel_rhs: bfloat16 [2, 8192, 128], P(None, 'row'), may hold values from -6 to 6
- below: bfloat16 [2, 22528, 8192], P(None, 'row', 'col'), may hold values from -0.03125 to 0.03125
- row_ids: int32 [2, 176], P(None, 'row'), may hold values from 0 to 256, as said below
- ancestor_rhs: bfloat16 [24576, 128], P(('row', 'col')), may hold values from -6 to 6
- ancestor_solution: bfloat16 [24576, 128], P(('row', 'col')), may hold values from -6 to 6
Outputs:
- solution: bfloat16 [2, 8192, 128], P(None, ('row', 'col'))
- rhs_updated: bfloat16 [24576, 128], P(('row', 'col'))
Inputs may be any that keep to these rules, and one draw needn't show every extreme that they name: diag_inverse[p] is lower triangular with a positive diagonal. `row_ids`: slots 22 r to 22 r + 21 of either panel belong to the r-th index of row. Each holds 256 (empty) or a later block row that this index owns: for panel 0 a panel-1 block row in [r * 8, r * 8 + 8) or a value in [64 + r * 24, 64 + r * 24 + 24); for panel 1 only the latter. Live ids of one panel are distinct. In each panel some index of row has all 22 slots live.
All inputs are finite; a program needn't handle non-finite values.
Results may differ from a plain program's by a relative error of at most 0.017.
Values may be sent and summed in bfloat16 or wider, within the bound.
A program may use at most 128 MiB of HBM per device.

v0:
```python
import jax
import jax.numpy as jnp
from jax import lax
from jax.sharding import PartitionSpec as P

BS = 128
NRHS = 128
PW = 64
CAP = 22
NA_R = 24


def on_device(diag_inverse, panel_rhs, below, row_ids, ancestor_rhs, ancestor_solution):
    row_count = lax.axis_size("row")
    row_place = lax.axis_index("row")
    col_place = lax.axis_index("col")
    panel_rows = PW // row_count
    contract_first = (((0,), (0,)), ((), ()))

    def row_total(partial_sum):
        return lax.psum(partial_sum.astype(jnp.bfloat16), "row").astype(jnp.float32)

    def col_total(partial_sum):
        return lax.psum(partial_sum.astype(jnp.bfloat16), "col").astype(jnp.float32)

    def pick_panel(slot_ids):
        position = slot_ids - row_place * panel_rows
        return (position[:, None] == jnp.arange(panel_rows)[None, :]) & (slot_ids[:, None] < PW)

    def pick_later(slot_ids):
        position = slot_ids - PW - row_place * NA_R
        return position[:, None] == jnp.arange(NA_R)[None, :]

    def to_rows(picked, slot_sums):
        placed = jnp.einsum(
            "sk,sbn->kbn", picked.astype(jnp.float32), slot_sums, precision=lax.Precision.HIGHEST
        )
        return placed.reshape(-1, NRHS)

    def slot_values(picked, source_rows):
        return jnp.einsum(
            "sk,kbn->sbn",
            picked.astype(jnp.bfloat16),
            source_rows,
            preferred_element_type=jnp.float32,
        )

    def transpose_product(panel_index, values):
        flat_values = values.astype(jnp.bfloat16).reshape(CAP * BS, NRHS)
        return lax.dot_general(
            below[panel_index], flat_values, contract_first, preferred_element_type=jnp.float32
        )

    def solve_back(forward_part, back_sum, panel_index):
        back_rhs = (forward_part.astype(jnp.float32) - back_sum).astype(jnp.bfloat16)
        return lax.dot_general(
            diag_inverse[panel_index], back_rhs, contract_first, preferred_element_type=jnp.float32
        )

    forward_zero = row_total(
        jnp.dot(diag_inverse[0], panel_rhs[0], preferred_element_type=jnp.float32)
    ).astype(jnp.bfloat16)
    slot_zero = jnp.dot(below[0], forward_zero, preferred_element_type=jnp.float32).reshape(
        CAP, BS, NRHS
    )
    panel_part = col_total(to_rows(pick_panel(row_ids[0]), slot_zero))
    panel_one_rhs = (panel_rhs[1].astype(jnp.float32) - panel_part).astype(jnp.bfloat16)
    forward_one = row_total(
        jnp.dot(diag_inverse[1], panel_one_rhs, preferred_element_type=jnp.float32)
    ).astype(jnp.bfloat16)
    later_zero = to_rows(pick_later(row_ids[0]), slot_zero)
    slot_one = jnp.dot(below[1], forward_one, preferred_element_type=jnp.float32).reshape(
        CAP, BS, NRHS
    )
    later_one = to_rows(pick_later(row_ids[1]), slot_one)

    def ancestor_share(partial_sum):
        return lax.psum_scatter(
            partial_sum.astype(jnp.bfloat16), "col", scatter_dimension=0, tiled=True
        ).astype(jnp.float32)

    update = ancestor_share(later_zero) + ancestor_share(later_one)
    rhs_updated = (ancestor_rhs.astype(jnp.float32) - update).astype(jnp.bfloat16)
    known_rows = lax.all_gather(ancestor_solution, "col", axis=0, tiled=True).reshape(
        NA_R, BS, NRHS
    )
    later_two = transpose_product(1, slot_values(pick_later(row_ids[1]), known_rows))
    ancestors_zero = slot_values(pick_later(row_ids[0]), known_rows)
    back_one = lax.psum(later_two.astype(jnp.bfloat16), "row").astype(jnp.float32)
    solution_one = col_total(solve_back(forward_one, back_one, 1)).astype(jnp.bfloat16)
    one_blocks = solution_one.reshape(panel_rows, BS, NRHS)
    values_zero = ancestors_zero + slot_values(pick_panel(row_ids[0]), one_blocks)
    back_zero = row_total(transpose_product(0, values_zero))
    share_rows = lax.psum_scatter(
        solve_back(forward_zero, back_zero, 0).astype(jnp.bfloat16),
        "col",
        scatter_dimension=0,
        tiled=True,
    )
    share_size = share_rows.shape[0]
    one_share = lax.dynamic_slice_in_dim(solution_one, col_place * share_size, share_size, 0)
    solution = jnp.stack([share_rows, one_share])
    return (solution, rhs_updated)


def solution(mesh):
    in_specs = (
        P(None, "col", "row"),
        P(None, "row", None),
        P(None, "row", "col"),
        P(None, "row"),
        P(("row", "col"), None),
        P(("row", "col"), None),
    )
    out_specs = (P(None, ("row", "col"), None), P(("row", "col"), None))
    return jax.shard_map(
        on_device, mesh=mesh, in_specs=in_specs, out_specs=out_specs, check_vma=False
    )
```

profile of v0, /device:TPU:0, one launch (start us, length us, event | category | flops | bytes accessed | tf_op | source)
XLA Modules:
  0.0 420.0 jit_solution(17048211158153917995)
XLA Ops:
  7.2 0.0 all-reduce.7.cloned.1.call-start
  7.2 4.3 %fusion.30 = bf16[2048,128]{1,0:T(8,128)(2,1)} fusion(bf16[2,2048,1024]{2,1,0:T(8,128)(2,1)} %param.6, bf16[2,1024,128]{2,1,0:T(8,128)(2,1)} %param.7), kind=kOutput, calls=%fused_computation.26 | convolution fusion | flops 537133056 | bytes 4980736 | tf_op jit(solution)/shard_map/dot_general | solution.py:61
  11.5 0.0 all-reduce.7.cloned.1.call-update
  11.6 0.0 all-reduce.9.cloned.1.call-start
  11.6 10.1 %all_gather.3 = bf16[3072,128]{1,0:T(8,128)(2,1)S(1)} all-gather(bf16[768,128]{1,0:T(8,128)(2,1)S(1)} %copy-done.1), channel_id=1, replica_groups=mesh['row'=8,'col'=4] {'col'}, dimensions={0}, use_global_device_ids=true | all-gather | bytes 983040 | tf_op jit(solution)/shard_map/all_gather | solution.py:84
  21.7 0.7 convolution_convert_fusion
  22.4 0.1 copy.22
  22.6 64.5 %all-reduce.7.cloned.1.call-done = bf16[2048,128]{1,0:T(8,128)(2,1)} async-done(((bf16[2048,128]{1,0:T(8,128)(2,1)}), bf16[2048,128]{1,0:T(8,128)(2,1)}) %all-reduce.7.cloned.1.call-update) | async-done | bytes 524304 | tf_op jit(solution)/shard_map/psum | solution.py:21
  87.1 9.6 %fusion.20 = f32[2816,128]{0,1:T(8,128)} fusion(bf16[2048,128]{1,0:T(8,128)(2,1)} %all-reduce.7.cloned.1.call-done, bf16[2,2816,2048]{2,1,0:T(8,128)(2,1)} %param.8), kind=kOutput, calls=%fused_computation.20 | convolution fusion | flops 1476395008 | bytes 13500416 | tf_op jit(solution)/shard_map/dot_general | solution.py:63
  96.7 1.8 copy.17
  98.5 1.4 fusion.69
  99.9 0.7 copy.19
  100.7 0.0 all-reduce.15.cloned.1.call-start
  100.7 6.8 %fusion.45 = bf16[2048,128]{0,1:T(8,128)(2,1)} fusion(bf16[2816,128]{1,0:T(8,128)(2,1)S(1)} %bitcast.120, bf16[2,2816,2048]{2,1,0:T(8,128)(2,1)} %param.8), kind=kOutput, calls=%fused_computation.31 | convolution fusion | flops 1476657152 | bytes 12779520 | tf_op jit(solution)/shard_map/dot_general | solution.py:50
  107.6 24.7 %all-reduce.9.cloned.1.call-done = bf16[1024,128]{1,0:T(8,128)(2,1)} async-done(((bf16[1024,128]{1,0:T(8,128)(2,1)}), bf16[1024,128]{1,0:T(8,128)(2,1)}) %all-reduce.9.cloned.1.call-update) | async-done | bytes 262160 | tf_op jit(solution)/shard_map/psum | solution.py:24
  132.3 4.6 %fusion.42 = bf16[2048,128]{0,1:T(8,128)(2,1)} fusion(bf16[2,2048,1024]{2,1,0:T(8,128)(2,1)} %param.6, bf16[1024,128]{1,0:T(8,128)(2,1)} %all-reduce.9.cloned.1.call-done, bf16[2,1024,128]{2,1,0:T(8,128)(2,1)S(1)} %copy-done.3), kind=kOutput, calls=%fused_computation.30 | convolution fusion | flops 537657344 | bytes 5242880 | tf_op jit(solution)/shard_map/dot_general | solution.py:69
  137.0 0.0 all-reduce.11.cloned.1.call-start
  137.0 78.4 %all-reduce.15.cloned.1.call-done = (bf16[2048,128]{0,1:T(8,128)(2,1)}, bf16[2048,128]{0,1:T(8,128)(2,1)}) async-done(((bf16[2048,128]{0,1:T(8,128)(2,1)}, bf16[2048,128]{0,1:T(8,128)(2,1)}), (bf16[2048,128]{0,1:T(8,128)(2,1)}, bf16[2048,128]{0,1:T(8,128)(2,1)})) %all-reduce.15.cloned.1.call-update) | async-done | bytes 1048592 | tf_op jit(solution)/shard_map/psum | solution.py:89
  215.4 3.9 fusion.72
  219.3 0.0 all-reduce.11.cloned.1.call-update
  219.4 0.2 all-reduce.13.cloned.1.call-start
  219.6 31.8 %all-reduce.11.cloned.1.call-done = bf16[1024,128]{0,1:T(8,128)(2,1)} async-done(((bf16[1024,128]{0,1:T(8,128)(2,1)}), bf16[1024,128]{0,1:T(8,128)(2,1)}) %all-reduce.11.cloned.1.call-update) | async-done | bytes 262160 | tf_op jit(solution)/shard_map/psum | solution.py:24
  251.4 1.0 copy.35
  252.4 0.2 copy.23
  252.7 0.4 fusion.98
  253.1 0.7 add_convert_fusion
  253.8 0.1 copy.24
  254.0 9.7 %fusion.48 = bf16[2048,128]{1,0:T(8,128)(2,1)} fusion(bf16[2816,128]{1,0:T(8,128)(2,1)S(1)} %bitcast.121, bf16[2,2816,2048]{2,1,0:T(8,128)(2,1)} %param.8), kind=kOutput, calls=%fused_computation.32 | convolution fusion | flops 1476657152 | bytes 12779520 | tf_op jit(solution)/shard_map/dot_general | solution.py:50
  263.7 0.0 all-reduce.13.cloned.1.call-update
  263.8 0.0 reduce-scatter.4.cloned.1.call-start
  263.8 72.8 %all-reduce.13.cloned.1.call-done = bf16[2048,128]{1,0:T(8,128)(2,1)} async-done(((bf16[2048,128]{1,0:T(8,128)(2,1)}), bf16[2048,128]{1,0:T(8,128)(2,1)}) %all-reduce.13.cloned.1.call-update) | async-done | bytes 524304 | tf_op jit(solution)/shard_map/psum | solution.py:21
  336.6 3.8 fusion.75
  340.4 0.0 reduce-scatter.6.cloned.1.call-start
  340.5 1.6 fusion.57
  342.1 1.1 copy.26
  343.2 0.3 reduce-scatter.8.cloned.1.call-start
  343.5 6.8 %fusion.23 = f32[2816,128]{0,1:T(8,128)S(1)} fusion(bf16[2048,128]{0,1:T(8,128)(2,1)} %get-tuple-element.7, bf16[2,2816,2048]{2,1,0:T(8,128)(2,1)} %param.8), kind=kOutput, calls=%fused_computation.21 | convolution fusion | flops 1476395008 | bytes 13500416 | tf_op jit(solution)/shard_map/dot_general | solution.py:72
  350.3 0.4 copy.27
  350.7 1.6 fusion.60
  352.3 1.1 copy.29
  353.4 0.0 reduce-scatter.8.cloned.1.call-update
  353.4 0.8 dynamic-slice_bitcast_fusion
  354.3 5.5 %reduce-scatter.4.cloned.1.call-done = bf16[256,128]{0,1:T(8,128)(2,1)} async-done(((bf16[1024,128]{0,1:T(8,128)(2,1)}), bf16[256,128]{0,1:T(8,128)(2,1)}) %reduce-scatter.4.cloned.1.call-update) | async-done | bytes 65552 | tf_op jit(solution)/shard_map/reduce_scatter | solution.py:94
  359.8 0.9 pad_maximum_fusion
  360.6 0.8 copy.30
  361.4 24.2 %reduce-scatter.6.cloned.1.call-done = bf16[768,128]{1,0:T(8,128)(2,1)} async-done(((bf16[3072,128]{1,0:T(8,128)(2,1)}), bf16[768,128]{1,0:T(8,128)(2,1)}) %reduce-scatter.6.cloned.1.call-update) | async-done | bytes 196624 | tf_op jit(solution)/shard_map/reduce_scatter | solution.py:78
  385.6 25.8 %reduce-scatter.8.cloned.1.call-done = bf16[768,128]{1,0:T(8,128)(2,1)} async-done(((bf16[3072,128]{1,0:T(8,128)(2,1)}), bf16[768,128]{1,0:T(8,128)(2,1)}) %reduce-scatter.8.cloned.1.call-update) | async-done | bytes 196624 | tf_op jit(solution)/shard_map/reduce_scatter | solution.py:78
  411.3 1.8 subtract_convert_fusion.4
  (16 shorter events, 0.1 us)
Async XLA Ops:
  7.2 4.4 %copy-start.1 = (bf16[768,128]{1,0:T(8,128)(2,1)S(1)}, bf16[768,128]{1,0:T(8,128)(2,1)}, u32[]{:S(2)}) copy-start(bf16[768,128]{1,0:T(8,128)(2,1)} %param.11) | copy-start | bytes 589828
  7.2 14.6 %copy-start.2 = (s32[2,22]{1,0:T(2,128)S(1)}, s32[2,22]{1,0:T(2,128)}, u32[]{:S(2)}) copy-start(s32[2,22]{1,0:T(2,128)} %param.9) | copy-start | bytes 532
  7.2 79.9 %all-reduce.7.cloned.1.call-start = ((), (), s32[]{:S(2)}) async-start(), calls=%async_computation.3 | async-start | bytes 1048576 | tf_op jit(solution)/shard_map/psum | solution.py:21
  11.6 120.7 %all-reduce.9.cloned.1.call-start = ((), (), s32[]{:S(2)}) async-start(), calls=%async_computation.4 | async-start | bytes 524288 | tf_op jit(solution)/shard_map/psum | solution.py:24
  100.7 114.7 %all-reduce.15.cloned.1.call-start = ((), (), s32[]{:S(2)}) async-start(), calls=%async_computation.10 | async-start | bytes 2097152 | tf_op jit(solution)/shard_map/psum | solution.py:89
  100.7 31.6 %copy-start.3 = (bf16[2,1024,128]{2,1,0:T(8,128)(2,1)S(1)}, bf16[2,1024,128]{2,1,0:T(8,128)(2,1)}, u32[]{:S(2)}) copy-start(bf16[2,1024,128]{2,1,0:T(8,128)(2,1)} %param.7) | copy-start | bytes 1572868
  137.0 114.5 %all-reduce.11.cloned.1.call-start = ((), (), s32[]{:S(2)}) async-start(), calls=%async_computation.5 | async-start | bytes 524288 | tf_op jit(solution)/shard_map/psum | solution.py:24
  219.4 117.2 %all-reduce.13.cloned.1.call-start = ((), (), s32[]{:S(2)}) async-start(), calls=%async_computation.6 | async-start | bytes 1048576 | tf_op jit(solution)/shard_map/psum | solution.py:21
  254.0 82.6 %copy-start.4 = (bf16[2048,128]{1,0:T(8,128)(2,1)S(1)}, bf16[2048,128]{1,0:T(8,128)(2,1)}, u32[]{:S(2)}) copy-start(bf16[2048,128]{1,0:T(8,128)(2,1)} %all-reduce.7.cloned.1.call-done) | copy-start | bytes 1572868
  263.8 96.0 %reduce-scatter.4.cloned.1.call-start = ((), (), s32[]{:S(2)}) async-start(), calls=%async_computation.7 | async-start | bytes 327680 | tf_op jit(solution)/shard_map/reduce_scatter | solution.py:94
  340.4 45.1 %reduce-scatter.6.cloned.1.call-start = ((), (), s32[]{:S(2)}) async-start(), calls=%async_computation.8 | async-start | bytes 983040 | tf_op jit(solution)/shard_map/reduce_scatter | solution.py:78
  343.2 68.1 %reduce-scatter.8.cloned.1.call-start = ((), (), s32[]{:S(2)}) async-start(), calls=%async_computation.9 | async-start | bytes 983040 | tf_op jit(solution)/shard_map/reduce_scatter | solution.py:78
  350.3 61.1 %copy-start = (bf16[768,128]{1,0:T(8,128)(2,1)S(1)}, bf16[768,128]{1,0:T(8,128)(2,1)}, u32[]{:S(2)}) copy-start(bf16[768,128]{1,0:T(8,128)(2,1)} %param.10) | copy-start | bytes 589828
Sparse Core Ops, SparseCore 0:
  11.7 75.3 all-reduce.6
  100.8 31.4 all-reduce.8
  137.1 78.2 all-reduce.14
  219.5 31.9 all-reduce.10
  263.9 72.6 all-reduce.12
  340.5 19.2 reduce-scatter.3
  362.3 23.1 reduce-scatter.5
  388.1 23.1 reduce-scatter.7
where the time goes:
time: 420 us
  waiting for transfers between devices  328 us (78%)
  matrix products  56.1 us (13%)
  between operations  14.3 us (3%)
  blocking collectives  10.1 us (2%)
  local copies, waits for them, and re-layouts  8.26 us (2%)
    psum x2, waiting for transfers between devices, row_total(): return lax.psum(partial_sum.astype(jnp.bfloat16), 'row').astype(jnp.float32)  137 us
    psum x1, waiting for transfers between devices, on_device(): lax.psum(later_two.astype(jnp.bfloat16), 'row').astype(jnp.float32)  78.4 us
    psum x2, waiting for transfers between devices, col_total(): return lax.psum(partial_sum.astype(jnp.bfloat16), 'col').astype(jnp.float32)  56.6 us
    reduce_scatter x2, waiting for transfers between devices, ancestor_share(): lax.psum_scatter(partial_sum.astype(jnp.bfloat16), 'col', scatter_dimensi...  49.9 us
    dot_general x2, matrix products, transpose_product(): lax.dot_general(below[panel_index], flat_values, contract_first, preferre...  16.6 us
    all_gather x1, blocking collectives, on_device(): lax.all_gather(ancestor_solution, 'col', axis=0, tiled=True)  10.1 us
    dot_general x1, matrix products, on_device(): jnp.dot(below[0], forward_zero, preferred_element_type=jnp.float32)  9.59 us
  transfers between devices with their start and end apart: 8, of which 8 were waited for; matrix products, arithmetic and copies ran while one was open for 5% of the time, Pallas kernels for 0%

commit v1 on v0

v1 whole, which is shorter than its diff:
```python
import functools

import jax
import jax.numpy as jnp
from jax import lax
from jax.experimental import pallas as pl
from jax.experimental.pallas import tpu as pltpu
from jax.sharding import PartitionSpec as P

MESH = pl.DeviceIdType.MESH
BF = jnp.bfloat16
F32 = jnp.float32


def sizes_of(n, m, diag, panel_rhs, below, row_ids, ancestor_rhs):
    z = {}
    z["n"], z["m"] = n, m
    z["nz"] = n // 2
    z["cc"], z["p"] = diag.shape[1], diag.shape[2]
    z["nrhs"] = panel_rhs.shape[2]
    z["cap"] = row_ids.shape[1]
    z["bs"] = below.shape[1] // z["cap"]
    z["b"] = z["cc"] // n
    z["q"] = z["p"] // m
    z["a"] = ancestor_rhs.shape[0]
    z["ab"] = z["a"] // z["bs"]
    z["na"] = z["ab"] * m
    z["pb"] = z["p"] // z["bs"]
    z["pw"] = z["cc"] * m // z["bs"]
    return z


def kernel(
    z, idx, d_hbm, prhs, b_hbm, arhs, asol, sol, upd,
    vd0, vd1, vb0, vb1, bp, known, vt, slots, accT,
    part_f0, part_b1, part_f1, part_b0, full_f0, full_b1, full_f1, full_b0,
    xr, zs, zr, part_p, full_p, part_s1, full_s1, part_s0, part_u, cr, cru,
    lsem, ssem, rsem,
):
    n, m, nz, b, q = z["n"], z["m"], z["nz"], z["b"], z["q"]
    cc, cap, bs, nrhs, na, pb = z["cc"], z["cap"], z["bs"], z["nrhs"], z["na"], z["pb"]
    ab, a = z["ab"], z["a"]
    me = lax.axis_index("row")
    mc = lax.axis_index("col")
    par = lax.rem(me, 2)
    zi = me // 2
    partner = me + 1 - 2 * par
    o_pan, o_l0, o_l1, o_p0, o_p1 = 0, pb, pb + na, pb + 2 * na, pb + 2 * na + cap

    counter = [0]
    pending = []

    def send(src, dst, axis, place, slot):
        cp = pltpu.make_async_remote_copy(
            src_ref=src, dst_ref=dst, send_sem=ssem.at[slot], recv_sem=rsem.at[slot],
            device_id={axis: place}, device_id_type=MESH,
        )
        cp.start()
        pending.append(cp)
        return cp

    def take(count):
        base = counter[0]
        counter[0] += count
        return base

    def rows(ref, block, size):
        return ref.at[pl.ds(pl.multiple_of(block * size, size), size)]

    def get(ref, block, size):
        return ref[pl.ds(pl.multiple_of(block * size, size), size), :]

    def put(ref, block, size, value):
        ref[pl.ds(pl.multiple_of(block * size, size), size), :] = value

    class RowSum:
        def __init__(self, which, part):
            self.w, self.part = which, part
            self.xs, self.zs = take(nz), take(nz)
            self.xc, self.zc = {}, {}

        def send_x(self, j):
            zd = lax.rem(zi + j, nz)
            self.xc[j] = send(
                rows(self.part, zd * 2 + 1 - par, b), xr.at[self.w, j], "row", partner, self.xs + j
            )

        def forward(self):
            for j in range(1, nz):
                zd = lax.rem(zi + j, nz)
                self.xc[j].wait_recv()
                both = get(self.part, zd * 2 + par, b).astype(F32) + xr[self.w, j].astype(F32)
                zs[self.w, j] = both.astype(BF)
                self.zc[j] = send(
                    zs.at[self.w, j], zr.at[self.w, j], "row", zd * 2 + par, self.zs + j
                )

        def finish(self):
            self.xc[0].wait_recv()
            total = get(self.part, me, b).astype(F32) + xr[self.w, 0].astype(F32)
            for j in range(1, nz):
                self.zc[j].wait_recv()
                total = total + zr[self.w, j].astype(F32)
            return total

    class RowGather:
        def __init__(self, full):
            self.full = full
            self.xs, self.zs = take(nz), take(nz)
            self.xc, self.zc = {}, {}

        def start(self):
            mine = rows(self.full, me, b)
            self.xc[0] = send(mine, mine, "row", partner, self.xs)
            for j in range(1, nz):
                self.zc[j] = send(mine, mine, "row", lax.rem(zi + j, nz) * 2 + par, self.zs + j)

        def forward(self):
            for j in range(1, nz):
                self.zc[j].wait_recv()
                theirs = rows(self.full, lax.rem(zi + nz - j, nz) * 2 + par, b)
                self.xc[j] = send(theirs, theirs, "row", partner, self.xs + j)

        def finish(self):
            for j in range(nz):
                self.xc[j].wait_recv()

    class ColSum:
        def __init__(self, part, landing, size):
            self.part, self.landing, self.size = part, landing, size
            self.s = take(m)
            self.c = {}

        def start(self):
            for d in range(1, m):
                place = lax.rem(mc + d, m)
                self.c[d] = send(
                    rows(self.part, place, self.size), self.landing.at[d], "col", place, self.s + d
                )

        def finish(self):
            total = get(self.part, mc, self.size).astype(F32)
            for d in range(1, m):
                self.c[d].wait_recv()
                total = total + self.landing[d].astype(F32)
            return total

    class ColGather:
        def __init__(self, src, dst):
            self.src, self.dst = src, dst
            self.s = take(m)
            self.c = {}

        def start(self):
            for d in range(1, m):
                self.c[d] = send(self.src, self.dst, "col", lax.rem(mc + d, m), self.s + d)

        def finish(self):
            for d in range(1, m):
                self.c[d].wait_recv()

    load_d0 = pltpu.make_async_copy(d_hbm.at[0], vd0, lsem.at[0])
    load_b1 = pltpu.make_async_copy(b_hbm.at[1], vb1, lsem.at[1])
    load_b0 = pltpu.make_async_copy(b_hbm.at[0], vb0.at[pl.ds(0, cap)], lsem.at[2])
    load_d1 = pltpu.make_async_copy(d_hbm.at[1], vd1, lsem.at[3])
    for load in (load_d0, load_b1, load_b0, load_d1):
        load.start()

    barrier = pltpu.get_barrier_semaphore()
    peers = [{"row": partner}]
    peers += [{"row": lax.rem(zi + j, nz) * 2 + par} for j in range(1, nz)]
    peers += [{"col": lax.rem(mc + d, m)} for d in range(1, m)]
    for peer in peers:
        pl.semaphore_signal(barrier, inc=1, device_id=peer, device_id_type=MESH)
    pl.semaphore_wait(barrier, len(peers))

    gather_a = ColGather(asol, known.at[pl.ds(mc * ab, ab)])
    gather_a.start()

    def solve_forward(summing, vd, x):
        order = list(range(1, nz)) + [0]
        for j in order:
            block = lax.rem(zi + j, nz) * 2 + 1 - par
            value = jnp.dot(get(vd, block, b), x, preferred_element_type=F32)
            put(summing.part, block, b, value.astype(BF))
            summing.send_x(j)
        for j in order:
            block = lax.rem(zi + j, nz) * 2 + par
            value = jnp.dot(get(vd, block, b), x, preferred_element_type=F32)
            put(summing.part, block, b, value.astype(BF))

    sum_f0 = RowSum(0, part_f0)
    load_d0.wait()
    solve_forward(sum_f0, vd0, prhs[0])
    known[pl.ds(mc * ab, ab)] = asol[...]
    known[na] = jnp.zeros((bs, nrhs), BF)
    vb0[cap] = jnp.zeros((bs, cc), BF)
    slots[0, cap] = jnp.zeros((bs, nrhs), F32)
    slots[1, cap] = jnp.zeros((bs, nrhs), F32)
    sum_f0.forward()
    load_b0.wait()
    for k in range(pb):
        bp[k] = vb0[idx[o_pan + k]]
    f0_mine = sum_f0.finish().astype(BF)
    put(full_f0, me, b, f0_mine)
    gather_f0 = RowGather(full_f0)
    gather_f0.start()

    def gather_values(offset):
        for s in range(cap):
            block = known[idx[offset + s]].astype(F32)
            vt[:, s * bs:(s + 1) * bs] = block.T.astype(BF)

    tile = min(256, cc)
    tiles = cc // tile

    load_b1.wait()
    gather_a.finish()
    gather_values(o_p1)

    def back_tile(vb, t):
        cols = pl.ds(pl.multiple_of(t * tile, tile), tile)
        return jnp.dot(
            vt[...], vb[0:cap, :, cols].reshape(cap * bs, tile), preferred_element_type=F32
        )

    def one_tile(t, carry):
        put(part_b1, t, tile, back_tile(vb1, t).T.astype(BF))
        return carry

    lax.fori_loop(0, tiles // 2, one_tile, 0)
    gather_f0.forward()
    lax.fori_loop(tiles // 2, tiles, one_tile, 0)
    gather_f0.finish()

    sum_p = ColSum(part_p, cr.at[0], q)
    panel_tile = 2 if pb % 2 == 0 else 1

    def panel_step(t, carry):
        block = bp[pl.ds(t * panel_tile, panel_tile)].reshape(panel_tile * bs, cc)
        value = jnp.dot(block, full_f0[...], preferred_element_type=F32)
        put(part_p, t, panel_tile * bs, value.astype(BF))
        return carry

    lax.fori_loop(0, pb // panel_tile, panel_step, 0)
    sum_p.start()
    sum_b1 = RowSum(1, part_b1)
    for j in list(range(1, nz)) + [0]:
        sum_b1.send_x(j)
    p_part = sum_p.finish()
    p_rhs = prhs[1, pl.ds(pl.multiple_of(mc * q, q), q), :].astype(F32)
    put(full_p, mc, q, (p_rhs - p_part).astype(BF))
    gather_p = ColGather(rows(full_p, mc, q), rows(full_p, mc, q))
    gather_p.start()
    sum_b1.forward()
    load_d1.wait()
    gather_p.finish()

    sum_f1 = RowSum(2, part_f1)
    solve_forward(sum_f1, vd1, full_p[...])
    sum_f1.forward()
    gather_values(o_p0)

    def zero_tile(t, carry):
        accT[:, pl.ds(pl.multiple_of(t * tile, tile), tile)] = back_tile(vb0, t)
        return carry

    lax.fori_loop(0, tiles, zero_tile, 0)
    b1_mine = sum_b1.finish()
    f1_mine = sum_f1.finish().astype(BF)
    put(full_b1, me, b, (f1_mine.astype(F32) - b1_mine).astype(BF))
    gather_b1 = RowGather(full_b1)
    gather_b1.start()
    put(full_f1, me, b, f1_mine)
    gather_b1.forward()
    gather_f1 = RowGather(full_f1)
    gather_f1.start()
    gather_b1.finish()

    def solve_back(full, vd, part):
        xt = full[...].astype(F32).T.astype(BF)
        yt = jnp.dot(xt, vd[...], preferred_element_type=F32)
        part[...] = yt.T.astype(BF)

    sum_s1 = ColSum(part_s1, cr.at[1], q)
    solve_back(full_b1, vd1, part_s1)
    sum_s1.start()
    gather_f1.forward()
    s1_mine = sum_s1.finish().astype(BF)
    put(full_s1, mc, q, s1_mine)
    gather_s1 = ColGather(rows(full_s1, mc, q), rows(full_s1, mc, q))
    gather_s1.start()
    sol[1] = s1_mine
    gather_s1.finish()

    s1t = full_s1[...].astype(F32).T.astype(BF)
    vt[:, 0:pb * bs] = s1t

    def panel_back(t, carry):
        cols = pl.ds(pl.multiple_of(t * tile, tile), tile)
        value = jnp.dot(
            vt[:, 0:pb * bs], bp[:, :, cols].reshape(pb * bs, tile), preferred_element_type=F32
        )
        put(part_b0, t, tile, (value + accT[:, cols]).T.astype(BF))
        return carry

    lax.fori_loop(0, tiles, panel_back, 0)
    sum_b0 = RowSum(3, part_b0)
    for j in list(range(1, nz)) + [0]:
        sum_b0.send_x(j)
    group = 2 if cap % 2 == 0 else 1

    def later(which, vb, full):
        def step(t, carry):
            block = vb[pl.ds(t * group, group)].reshape(group * bs, cc)
            value = jnp.dot(block, full[...], preferred_element_type=F32)
            slots[which, pl.ds(t * group, group)] = value.reshape(group, bs, nrhs)
            return carry

        lax.fori_loop(0, cap // group, step, 0)

    sum_b0.forward()
    later(0, vb0, full_f0)
    b0_mine = sum_b0.finish()
    put(full_b0, me, b, (f0_mine.astype(F32) - b0_mine).astype(BF))
    gather_b0 = RowGather(full_b0)
    gather_b0.start()
    gather_b0.forward()
    gather_f1.finish()
    later(1, vb1, full_f1)
    for k in range(na):
        value = slots[0, idx[o_l0 + k]] + slots[1, idx[o_l1 + k]]
        part_u[k * bs:(k + 1) * bs, :] = value.astype(BF)
    gather_b0.finish()

    sum_s0 = ColSum(part_s0, cr.at[2], q)
    sum_u = ColSum(part_u, cru, a)
    solve_back(full_b0, vd0, part_s0)
    sum_s0.start()
    sum_u.start()
    sol[0] = sum_s0.finish().astype(BF)
    upd[...] = (arhs[...].astype(F32) - sum_u.finish()).astype(BF)
    for cp in pending:
        cp.wait_send()


def on_device(diag, panel_rhs, below, row_ids, ancestor_rhs, ancestor_solution):
    n, m = lax.axis_size("row"), lax.axis_size("col")
    z = sizes_of(n, m, diag, panel_rhs, below, row_ids, ancestor_rhs)
    nz, b, q = z["nz"], z["b"], z["q"]
    cc, p, cap, bs, nrhs, na, pb = (z[k] for k in ("cc", "p", "cap", "bs", "nrhs", "na", "pb"))
    a, ab = z["a"], z["ab"]
    row = lax.axis_index("row")

    def slot_of(ids, wanted):
        found = ids[None, :] == wanted[:, None]
        return jnp.min(jnp.where(found, jnp.arange(cap)[None, :], cap), axis=1)

    def place_of(ids):
        position = ids - z["pw"] - row * na
        return jnp.where((position >= 0) & (position < na), position, na)

    later_ids = z["pw"] + row * na + jnp.arange(na)
    idx = jnp.concatenate([
        slot_of(row_ids[0], row * pb + jnp.arange(pb)),
        slot_of(row_ids[0], later_ids),
        slot_of(row_ids[1], later_ids),
        place_of(row_ids[0]),
        place_of(row_ids[1]),
    ]).astype(jnp.int32)

    vmem = pl.BlockSpec(memory_space=pltpu.VMEM)
    hbm = pl.BlockSpec(memory_space=pl.ANY)
    nsem = 4 * 2 * nz + 4 * 2 * nz + 7 * m
    V = pltpu.VMEM
    return pl.pallas_call(
        functools.partial(kernel, z),
        out_shape=(
            jax.ShapeDtypeStruct((2, q, nrhs), BF),
            jax.ShapeDtypeStruct((a, nrhs), BF),
        ),
        in_specs=[pl.BlockSpec(memory_space=pltpu.SMEM), hbm, vmem, hbm, vmem, vmem],
        out_specs=(vmem, vmem),
        scratch_shapes=[
            V((cc, p), BF), V((cc, p), BF),
            V((cap + 1, bs, cc), BF), V((cap, bs, cc), BF), V((pb, bs, cc), BF),
            V((na + 1, bs, nrhs), BF), V((nrhs, max(cap, pb) * bs), BF),
            V((2, cap + 1, bs, nrhs), F32), V((nrhs, cc), F32),
        ] + [V((cc, nrhs), BF)] * 8 + [V((4, nz, b, nrhs), BF)] * 3 + [
            V((p, nrhs), BF), V((p, nrhs), BF), V((p, nrhs), BF), V((p, nrhs), BF),
            V((p, nrhs), BF), V((na * bs, nrhs), BF),
            V((3, m, q, nrhs), BF), V((m, a, nrhs), BF),
            pltpu.SemaphoreType.DMA((4,)),
            pltpu.SemaphoreType.DMA((nsem,)),
            pltpu.SemaphoreType.DMA((nsem,)),
        ],
        compiler_params=pltpu.CompilerParams(
            collective_id=0, has_side_effects=True, vmem_limit_bytes=62 * 1024 * 1024
        ),
    )(
        idx, diag, panel_rhs, below.reshape(2, cap, bs, cc), ancestor_rhs,
        ancestor_solution.reshape(ab, bs, nrhs),
    )


def solution(mesh):
    in_specs = (
        P(None, "col", "row"),
        P(None, "row", None),
        P(None, "row", "col"),
        P(None, "row"),
        P(("row", "col"), None),
        P(("row", "col"), None),
    )
    out_specs = (P(None, ("row", "col"), None), P(("row", "col"), None))
    return jax.shard_map(
        on_device, mesh=mesh, in_specs=in_specs, out_specs=out_specs, check_vma=False
    )
```

time: 420 us -> 119 us (0.28)
  waiting for transfers between devices: 328 us -> 0 us
  Pallas kernels: 0 us -> 111 us
  matrix products: 56.1 us -> 0 us
  between operations: 14.3 us -> 0.66 us
  blocking collectives: 10.1 us -> 0 us
    psum x5 -> x0, waiting for transfers between devices: 272 us -> none  [the longest x2 137 us: row_total(): return lax.psum(partial_sum.astype(jnp.bfloat16), 'row').astype(jnp.float32)]
    pallas_call x0 -> x1, Pallas kernels: none -> 111 us  [on_device(): pl.pallas_call(functools.partial(kernel, z), out_shape=(jax.ShapeDtypeStr...]
    dot_general x14 -> x0, matrix products: 56.1 us -> none  [the longest x2 16.6 us: transpose_product(): lax.dot_general(below[panel_index], flat_values, contract_first, preferre...]
    reduce_scatter x3 -> x0, waiting for transfers between devices: 55.4 us -> none  [the longest x2 49.9 us: ancestor_share(): lax.psum_scatter(partial_sum.astype(jnp.bfloat16), 'col', scatter_dimensi...]
    all_gather x1 -> x0, blocking collectives: 10.1 us -> none  [on_device(): lax.all_gather(ancestor_solution, 'col', axis=0, tiled=True)]
  transfers between devices with their start and end apart: 8 -> 0, of which waited for: 8 -> 0; matrix products, arithmetic and copies ran while one was open for 5% -> 0% of each run, Pallas kernels for 0% -> 0%
where the time goes in v1:
time: 119 us; the launch traced here: 117 us
  Pallas kernels  111 us (93%)
  local copies, waits for them, and re-layouts  4.54 us (4%)
    pallas_call x1, Pallas kernels, on_device(): pl.pallas_call(functools.partial(kernel, z), out_shape=(jax.ShapeDtypeStr...  111 us
    unnamed x2, local copies, waits for them, and re-layouts  3.18 us

profile of v1, /device:TPU:0, one launch (start us, length us, event | category | flops | bytes accessed | tf_op | source)
XLA Modules:
  0.0 116.9 jit_solution(9067833475976587835)
XLA Ops:
  0.7 0.8 and_select_fusion
  1.4 0.8 slice_bitcast_fusion
  2.2 0.2 select_reduce_fusion.2
  2.4 0.1 select_reduce_fusion
  2.5 0.6 concatenate.3.idx
  3.1 110.6 %shard_map.77 = (bf16[2,256,128]{2,1,0:T(8,128)(2,1)}, bf16[768,128]{1,0:T(8,128)(2,1)}) custom-call(s32[100]{0:T(128)} %concatenate.3.idx, bf16[2,2048,1024]{2,1,0:T(8,128)(2,1)} %d_hbm.1, bf16[2,1024,128]{2,1,0:T(8,128)(2,1)} %prhs.1, bf16[2,22,128,2048]{3,2,1,0:T(8,128)(2,1)} %bitcast.10, bf16[768,128]{1,0:T(8,128)(2,1)} %arhs.1, ...), custom_call_target="tpu_custom_call" | custom-call | tf_op jit(solution)/shard_map/pallas_call | solution.py:376
  113.7 1.6 %copy.10 = bf16[2,256,128]{2,1,0:T(8,128)(2,1)} copy(bf16[2,256,128]{2,1,0:T(8,128)(2,1)} %get-tuple-element.10) | data formatting | bytes 262144
  115.3 1.6 %copy.11 = bf16[768,128]{1,0:T(8,128)(2,1)} copy(bf16[768,128]{1,0:T(8,128)(2,1)} %get-tuple-element.11) | data formatting | bytes 393216
  (2 shorter events, 0.0 us)

commit v2 on v1

v2 whole, which is shorter than its diff:
```python
import functools

import jax
import jax.numpy as jnp
from jax import lax
from jax.experimental import pallas as pl
from jax.experimental.pallas import tpu as pltpu
from jax.sharding import PartitionSpec as P

MESH = pl.DeviceIdType.MESH
BF = jnp.bfloat16
F32 = jnp.float32


def sizes_of(n, m, diag, panel_rhs, below, row_ids, ancestor_rhs):
    z = {}
    z["n"], z["m"] = n, m
    z["nz"] = n // 2
    z["cc"], z["p"] = diag.shape[1], diag.shape[2]
    z["nrhs"] = panel_rhs.shape[2]
    z["cap"] = row_ids.shape[1]
    z["bs"] = below.shape[1] // z["cap"]
    z["b"] = z["cc"] // n
    z["q"] = z["p"] // m
    z["a"] = ancestor_rhs.shape[0]
    z["ab"] = z["a"] // z["bs"]
    z["na"] = z["ab"] * m
    z["pb"] = z["p"] // z["bs"]
    z["pw"] = z["cc"] * m // z["bs"]
    return z


def kernel(
    z, idx, d_hbm, prhs, b_hbm, arhs, asol, sol, upd,
    vd0, vd1, vb0, vb1, bp, known, vt, slots, accT,
    part_b1, full_f1, wide, part_f0, part_f1, part_b0, full_f0, full_b1, full_b0,
    xr, zs, zr, xr1, zs1, zr1, part_p, full_p, part_s1, full_s1, part_s0, part_u, cr, cru,
    lsem, ssem, rsem,
):
    n, m, nz, b, q = z["n"], z["m"], z["nz"], z["b"], z["q"]
    cc, cap, bs, nrhs, na, pb = z["cc"], z["cap"], z["bs"], z["nrhs"], z["na"], z["pb"]
    ab, a = z["ab"], z["a"]
    me = lax.axis_index("row")
    mc = lax.axis_index("col")
    par = lax.rem(me, 2)
    zi = me // 2
    partner = me + 1 - 2 * par
    o_pan, o_l0, o_l1, o_p0, o_p1 = 0, pb, pb + na, pb + 2 * na, pb + 2 * na + cap

    counter = [0]
    pending = []

    def send(src, dst, axis, place, slot):
        cp = pltpu.make_async_remote_copy(
            src_ref=src, dst_ref=dst, send_sem=ssem.at[slot], recv_sem=rsem.at[slot],
            device_id={axis: place}, device_id_type=MESH,
        )
        cp.start()
        pending.append(cp)
        return cp

    def take(count):
        base = counter[0]
        counter[0] += count
        return base

    def rows(ref, block, size):
        return ref.at[pl.ds(pl.multiple_of(block * size, size), size)]

    def get(ref, block, size):
        return ref[pl.ds(pl.multiple_of(block * size, size), size), :]

    def put(ref, block, size, value):
        ref[pl.ds(pl.multiple_of(block * size, size), size), :] = value

    class RowSum:
        def __init__(self, part, size, xr, zs, zr):
            self.part, self.size = part, size
            self.xr, self.zs, self.zr = xr, zs, zr
            self.xk, self.zk = take(nz), take(nz)
            self.xc, self.zc = {}, {}

        def send_x(self, j):
            zd = lax.rem(zi + j, nz)
            self.xc[j] = send(
                rows(self.part, zd * 2 + 1 - par, self.size), self.xr.at[j], "row", partner,
                self.xk + j,
            )

        def forward(self):
            for j in range(1, nz):
                zd = lax.rem(zi + j, nz)
                self.xc[j].wait_recv()
                mine = get(self.part, zd * 2 + par, self.size)
                self.zs[j] = (mine.astype(F32) + self.xr[j].astype(F32)).astype(BF)
                self.zc[j] = send(
                    self.zs.at[j], self.zr.at[j], "row", zd * 2 + par, self.zk + j
                )

        def finish(self):
            self.xc[0].wait_recv()
            total = get(self.part, me, self.size).astype(F32) + self.xr[0].astype(F32)
            for j in range(1, nz):
                self.zc[j].wait_recv()
                total = total + self.zr[j].astype(F32)
            return total

    class RowGather:
        def __init__(self, full, size):
            self.full, self.size = full, size
            self.xk, self.zk = take(nz), take(nz)
            self.xc, self.zc = {}, {}

        def start(self):
            mine = rows(self.full, me, self.size)
            self.xc[0] = send(mine, mine, "row", partner, self.xk)
            for j in range(1, nz):
                self.zc[j] = send(mine, mine, "row", lax.rem(zi + j, nz) * 2 + par, self.zk + j)

        def forward(self):
            for j in range(1, nz):
                self.zc[j].wait_recv()
                theirs = rows(self.full, lax.rem(zi + nz - j, nz) * 2 + par, self.size)
                self.xc[j] = send(theirs, theirs, "row", partner, self.xk + j)

        def finish(self):
            for j in range(nz):
                self.xc[j].wait_recv()

    class ColSum:
        def __init__(self, part, landing, size):
            self.part, self.landing, self.size = part, landing, size
            self.s = take(m)
            self.c = {}

        def start(self):
            for d in range(1, m):
                place = lax.rem(mc + d, m)
                self.c[d] = send(
                    rows(self.part, place, self.size), self.landing.at[d], "col", place, self.s + d
                )

        def finish(self):
            total = get(self.part, mc, self.size).astype(F32)
            for d in range(1, m):
                self.c[d].wait_recv()
                total = total + self.landing[d].astype(F32)
            return total

    class ColGather:
        def __init__(self, src, dst):
            self.src, self.dst = src, dst
            self.s = take(m)
            self.c = {}

        def start(self):
            for d in range(1, m):
                self.c[d] = send(self.src, self.dst, "col", lax.rem(mc + d, m), self.s + d)

        def finish(self):
            for d in range(1, m):
                self.c[d].wait_recv()

    load_d0 = pltpu.make_async_copy(d_hbm.at[0], vd0, lsem.at[0])
    load_b1 = pltpu.make_async_copy(b_hbm.at[1], vb1, lsem.at[1])
    load_b0 = pltpu.make_async_copy(b_hbm.at[0], vb0.at[pl.ds(0, cap)], lsem.at[2])
    load_d1 = pltpu.make_async_copy(d_hbm.at[1], vd1, lsem.at[3])
    for load in (load_d0, load_b1, load_b0, load_d1):
        load.start()

    barrier = pltpu.get_barrier_semaphore()
    peers = [{"row": partner}]
    peers += [{"row": lax.rem(zi + j, nz) * 2 + par} for j in range(1, nz)]
    peers += [{"col": lax.rem(mc + d, m)} for d in range(1, m)]
    for peer in peers:
        pl.semaphore_signal(barrier, inc=1, device_id=peer, device_id_type=MESH)
    pl.semaphore_wait(barrier, len(peers))

    gather_a = ColGather(asol, known.at[pl.ds(mc * ab, ab)])
    gather_a.start()

    hb, hq, hn = b // 2, q // 2, nrhs // 2

    def pack(value, size):
        blocks = value.reshape(-1, size, hn)
        half = size // 2
        both = jnp.concatenate([blocks[:, :half], blocks[:, half:]], axis=2)
        return both.reshape(-1, nrhs)

    def unpack(value, size):
        half = size // 2
        blocks = value.astype(F32).reshape(-1, half, nrhs)
        both = jnp.concatenate([blocks[:, :, :hn], blocks[:, :, hn:]], axis=1)
        return both.reshape(-1, hn)

    def part_of(value, h):
        return value[:, h * hn:(h + 1) * hn]

    order = list(range(1, nz)) + [0]
    tile = max(min(256, cc), b)
    tiles = cc // tile

    sum_f0 = [RowSum(part_f0.at[h], hb, xr.at[0, h], zs.at[0, h], zr.at[0, h]) for h in range(2)]
    sum_f1 = [RowSum(part_f1.at[h], hb, xr.at[1, h], zs.at[1, h], zr.at[1, h]) for h in range(2)]
    sum_b0 = [RowSum(part_b0.at[h], hb, xr.at[2, h], zs.at[2, h], zr.at[2, h]) for h in range(2)]
    sum_b1 = RowSum(part_b1, b, xr1, zs1, zr1)
    gather_f0 = [RowGather(full_f0.at[h], hb) for h in range(2)]
    gather_b1 = [RowGather(full_b1.at[h], hb) for h in range(2)]
    gather_b0 = [RowGather(full_b0.at[h], hb) for h in range(2)]
    gather_f1 = RowGather(full_f1, b)
    sum_p = [ColSum(part_p.at[h], cr.at[0, h], hq) for h in range(2)]
    sum_s1 = [ColSum(part_s1.at[h], cr.at[1, h], hq) for h in range(2)]
    sum_s0 = [ColSum(part_s0.at[h], cr.at[2, h], hq) for h in range(2)]
    sum_u = ColSum(part_u, cru, a)

    def col_gather(full, h):
        mine = rows(full.at[h], mc, hq)
        return ColGather(mine, mine)

    gather_p = [col_gather(full_p, h) for h in range(2)]
    gather_s1 = [col_gather(full_s1, h) for h in range(2)]

    load_d0.wait()
    x0 = prhs[0]
    for j in order:
        block = lax.rem(zi + j, nz) * 2 + 1 - par
        value = jnp.dot(get(vd0, block, b), x0, preferred_element_type=F32)
        for h in range(2):
            put(part_f0.at[h], block, hb, pack(part_of(value, h), b).astype(BF))
        sum_f0[0].send_x(j)
    for j in order:
        sum_f0[1].send_x(j)
    for j in order:
        block = lax.rem(zi + j, nz) * 2 + par
        value = jnp.dot(get(vd0, block, b), x0, preferred_element_type=F32)
        for h in range(2):
            put(part_f0.at[h], block, hb, pack(part_of(value, h), b).astype(BF))
    known[pl.ds(mc * ab, ab)] = asol[...]
    known[na] = jnp.zeros((bs, nrhs), BF)
    vb0[cap] = jnp.zeros((bs, cc), BF)
    slots[0, cap] = jnp.zeros((bs, nrhs), F32)
    slots[1, cap] = jnp.zeros((bs, nrhs), F32)

    def gather_values(offset):
        for s in range(cap):
            block = known[idx[offset + s]].astype(F32)
            vt[:, s * bs:(s + 1) * bs] = block.T.astype(BF)

    def back_tile(vb, t):
        cols = pl.ds(pl.multiple_of(t * tile, tile), tile)
        return jnp.dot(
            vt[:, 0:cap * bs], vb[0:cap, :, cols].reshape(cap * bs, tile),
            preferred_element_type=F32,
        )

    def one_tile(t, carry):
        put(part_b1, t, tile, back_tile(vb1, t).T.astype(BF))
        return carry

    def zero_tile(t, carry):
        accT[:, pl.ds(pl.multiple_of(t * tile, tile), tile)] = back_tile(vb0, t)
        return carry

    group = 2 if cap % 2 == 0 else 1

    def later(which, vb):
        def step(t, carry):
            block = vb[pl.ds(t * group, group)].reshape(group * bs, cc)
            value = jnp.dot(block, wide[which], preferred_element_type=F32)
            slots[which, pl.ds(t * group, group)] = value.reshape(group, bs, nrhs)
            return carry

        lax.fori_loop(0, cap // group, step, 0)

    def solve_forward(summing, h, vd, x):
        for j in order:
            block = lax.rem(zi + j, nz) * 2 + 1 - par
            value = jnp.dot(get(vd, block, b), x, preferred_element_type=F32)
            put(summing.part, block, hb, pack(value, b).astype(BF))
            summing.send_x(j)
        for j in order:
            block = lax.rem(zi + j, nz) * 2 + par
            value = jnp.dot(get(vd, block, b), x, preferred_element_type=F32)
            put(summing.part, block, hb, pack(value, b).astype(BF))

    def solve_back(full, h, vd, part):
        xt = unpack(full[h], b).T.astype(BF)
        yt = jnp.dot(xt, vd[...], preferred_element_type=F32)
        part[h] = pack(yt.T, q).astype(BF)

    panel_tile = 2 if pb % 2 == 0 else 1
    held = {}

    def chain(h):
        sum_f0[h].forward()
        yield
        f0_mine = sum_f0[h].finish().astype(BF)
        put(full_f0.at[h], me, hb, f0_mine)
        gather_f0[h].start()
        yield
        gather_f0[h].forward()
        yield
        gather_f0[h].finish()
        x = unpack(full_f0[h], b).astype(BF)
        held["f0", h] = x

        for t in range(pb // panel_tile):
            block = bp[t * panel_tile:(t + 1) * panel_tile].reshape(panel_tile * bs, cc)
            value = jnp.dot(block, x, preferred_element_type=F32)
            put(part_p.at[h], t, panel_tile * bs // 2, pack(value, q).astype(BF))
        sum_p[h].start()
        yield
        p_part = sum_p[h].finish()
        mine = prhs[1, pl.ds(pl.multiple_of(mc * q, q), q), :].astype(F32)
        put(full_p.at[h], mc, hq, (pack(part_of(mine, h), q) - p_part).astype(BF))
        gather_p[h].start()
        yield
        gather_p[h].finish()
        solve_forward(sum_f1[h], h, vd1, unpack(full_p[h], q).astype(BF))
        yield
        sum_f1[h].forward()
        yield
        f1_mine = sum_f1[h].finish().astype(BF)
        put(full_b1.at[h], me, hb, (f1_mine.astype(F32) - held["b1"][h]).astype(BF))
        gather_b1[h].start()
        put(full_f1, me * 2 + h, hb, f1_mine)
        yield
        gather_b1[h].forward()
        yield
        gather_b1[h].finish()
        solve_back(full_b1, h, vd1, part_s1)
        sum_s1[h].start()
        yield
        put(full_s1.at[h], mc, hq, sum_s1[h].finish().astype(BF))
        gather_s1[h].start()
        yield
        gather_s1[h].finish()
        s1t = unpack(full_s1[h], q).T.astype(BF)
        for t in range(tiles):
            cols = slice(t * tile, (t + 1) * tile)
            value = jnp.dot(
                s1t, bp[:, :, cols].reshape(pb * bs, tile), preferred_element_type=F32
            )
            value = (value + accT[h * hn:(h + 1) * hn, cols]).T
            put(part_b0.at[h], t, tile // 2, pack(value, b).astype(BF))
        for j in order:
            sum_b0[h].send_x(j)
        yield
        sum_b0[h].forward()
        yield
        b0_mine = sum_b0[h].finish()
        put(full_b0.at[h], me, hb, (f0_mine.astype(F32) - b0_mine).astype(BF))
        gather_b0[h].start()
        yield
        gather_b0[h].forward()
        yield
        gather_b0[h].finish()
        solve_back(full_b0, h, vd0, part_s0)
        sum_s0[h].start()
        yield

    half_tiles = tiles // 2

    def beside_f0_sum():
        load_b0.wait()
        for k in range(pb):
            bp[k] = vb0[idx[o_pan + k]]

    def beside_f0_gather():
        load_b1.wait()
        gather_a.finish()
        gather_values(o_p1)
        lax.fori_loop(0, half_tiles, one_tile, 0)

    def rest_of_b1():
        lax.fori_loop(half_tiles, tiles, one_tile, 0)

    def send_b1():
        for j in order:
            sum_b1.send_x(j)
        wide[0] = jnp.concatenate([held["f0", 0], held["f0", 1]], axis=1)

    def forward_b1():
        sum_b1.forward()
        gather_values(o_p0)
        load_d1.wait()

    def first_ancestors():
        lax.fori_loop(0, half_tiles, zero_tile, 0)

    def rest_of_ancestors():
        lax.fori_loop(half_tiles, tiles, zero_tile, 0)
        total = sum_b1.finish()
        held["b1"] = [pack(part_of(total, h), b) for h in range(2)]

    def later_zero():
        later(0, vb0)

    def later_one():
        gather_f1.finish()
        blocks = full_f1[...].reshape(n, 2, hb, nrhs)
        wide[1] = jnp.concatenate(
            [unpack(blocks[:, h].reshape(n * hb, nrhs), b).astype(BF) for h in range(2)], axis=1
        )
        later(1, vb1)
        for k in range(na):
            value = slots[0, idx[o_l0 + k]] + slots[1, idx[o_l1 + k]]
            part_u[k * bs:(k + 1) * bs, :] = value.astype(BF)
        sum_u.start()

    beside = [
        beside_f0_sum, beside_f0_gather, rest_of_b1, send_b1, forward_b1, first_ancestors,
        rest_of_ancestors, later_zero, gather_f1.start, gather_f1.forward, None, None,
        later_one, None, None, None,
    ]
    chains = [chain(0), chain(1)]
    for extra in beside:
        for one in chains:
            next(one)
        if extra is not None:
            extra()

    for which, done in ((1, full_s1), (0, None)):
        halves = []
        for h in range(2):
            if done is None:
                packed = sum_s0[h].finish()
            else:
                packed = get(done.at[h], mc, hq)
            halves.append(unpack(packed, q).astype(BF))
        sol[which] = jnp.concatenate(halves, axis=1)
    upd[...] = (arhs[...].astype(F32) - sum_u.finish()).astype(BF)
    for cp in pending:
        cp.wait_send()


def on_device(diag, panel_rhs, below, row_ids, ancestor_rhs, ancestor_solution):
    n, m = lax.axis_size("row"), lax.axis_size("col")
    z = sizes_of(n, m, diag, panel_rhs, below, row_ids, ancestor_rhs)
    nz, b, q = z["nz"], z["b"], z["q"]
    cc, p, cap, bs, nrhs, na, pb = (z[k] for k in ("cc", "p", "cap", "bs", "nrhs", "na", "pb"))
    a, ab = z["a"], z["ab"]
    row = lax.axis_index("row")

    def slot_of(ids, wanted):
        found = ids[None, :] == wanted[:, None]
        return jnp.min(jnp.where(found, jnp.arange(cap)[None, :], cap), axis=1)

    def place_of(ids):
        position = ids - z["pw"] - row * na
        return jnp.where((position >= 0) & (position < na), position, na)

    later_ids = z["pw"] + row * na + jnp.arange(na)
    idx = jnp.concatenate([
        slot_of(row_ids[0], row * pb + jnp.arange(pb)),
        slot_of(row_ids[0], later_ids),
        slot_of(row_ids[1], later_ids),
        place_of(row_ids[0]),
        place_of(row_ids[1]),
    ]).astype(jnp.int32)

    vmem = pl.BlockSpec(memory_space=pltpu.VMEM)
    hbm = pl.BlockSpec(memory_space=pl.ANY)
    nsem = 14 * 2 * nz + 12 * m
    V = pltpu.VMEM
    return pl.pallas_call(
        functools.partial(kernel, z),
        out_shape=(
            jax.ShapeDtypeStruct((2, q, nrhs), BF),
            jax.ShapeDtypeStruct((a, nrhs), BF),
        ),
        in_specs=[pl.BlockSpec(memory_space=pltpu.SMEM), hbm, vmem, hbm, vmem, vmem],
        out_specs=(vmem, vmem),
        scratch_shapes=[
            V((cc, p), BF), V((cc, p), BF),
            V((cap + 1, bs, cc), BF), V((cap, bs, cc), BF), V((pb, bs, cc), BF),
            V((na + 1, bs, nrhs), BF), V((nrhs, max(cap, pb) * bs), BF),
            V((2, cap + 1, bs, nrhs), F32), V((nrhs, cc), F32),
            V((cc, nrhs), BF), V((cc, nrhs), BF), V((2, cc, nrhs), BF),
        ] + [V((2, cc // 2, nrhs), BF)] * 6 + [V((3, 2, nz, b // 2, nrhs), BF)] * 3 + [
            V((nz, b, nrhs), BF)
        ] * 3 + [V((2, p // 2, nrhs), BF)] * 5 + [
            V((na * bs, nrhs), BF),
            V((3, 2, m, q // 2, nrhs), BF), V((m, a, nrhs), BF),
            pltpu.SemaphoreType.DMA((4,)),
            pltpu.SemaphoreType.DMA((nsem,)),
            pltpu.SemaphoreType.DMA((nsem,)),
        ],
        compiler_params=pltpu.CompilerParams(
            collective_id=0, has_side_effects=True, vmem_limit_bytes=62 * 1024 * 1024
        ),
    )(
        idx, diag, panel_rhs, below.reshape(2, cap, bs, cc), ancestor_rhs,
        ancestor_solution.reshape(ab, bs, nrhs),
    )


def solution(mesh):
    in_specs = (
        P(None, "col", "row"),
        P(None, "row", None),
        P(None, "row", "col"),
        P(None, "row"),
        P(("row", "col"), None),
        P(("row", "col"), None),
    )
    out_specs = (P(None, ("row", "col"), None), P(("row", "col"), None))
    return jax.shard_map(
        on_device, mesh=mesh, in_specs=in_specs, out_specs=out_specs, check_vma=False
    )
```

time: 119 us -> 105 us (0.88); the launches traced: 117 us -> 105 us
  Pallas kernels: 111 us -> 98.8 us
    pallas_call x1, Pallas kernels: 111 us -> 98.8 us  [on_device(): pl.pallas_call(functools.partial(kernel, z), out_shape=(jax.ShapeDtypeStr...]
where the time goes in v2:
time: 105 us
  Pallas kernels  98.8 us (94%)
  local copies, waits for them, and re-layouts  4.54 us (4%)
  other arithmetic  1.05 us (1%)
    pallas_call x1, Pallas kernels, on_device(): pl.pallas_call(functools.partial(kernel, z), out_shape=(jax.ShapeDtypeStr...  98.8 us
    unnamed x2, local copies, waits for them, and re-layouts  3.18 us

profile of v2, /device:TPU:0, one launch (start us, length us, event | category | flops | bytes accessed | tf_op | source)
XLA Modules:
  0.0 105.0 jit_solution(15676568548154930977)
XLA Ops:
  0.7 0.8 and_select_fusion
  1.4 0.8 slice_bitcast_fusion
  2.2 0.2 select_reduce_fusion.2
  2.4 0.1 select_reduce_fusion
  2.5 0.6 concatenate.3.idx
  3.1 98.8 %shard_map.77 = (bf16[2,256,128]{2,1,0:T(8,128)(2,1)}, bf16[768,128]{1,0:T(8,128)(2,1)}) custom-call(s32[100]{0:T(128)} %concatenate.3.idx, bf16[2,2048,1024]{2,1,0:T(8,128)(2,1)} %d_hbm.1, bf16[2,1024,128]{2,1,0:T(8,128)(2,1)} %prhs.1, bf16[2,22,128,2048]{3,2,1,0:T(8,128)(2,1)} %bitcast.10, bf16[768,128]{1,0:T(8,128)(2,1)} %arhs.1, ...), custom_call_target="tpu_custom_call" | custom-call | tf_op jit(solution)/shard_map/pallas_call | solution.py:466
  101.8 1.6 %copy.10 = bf16[2,256,128]{2,1,0:T(8,128)(2,1)} copy(bf16[2,256,128]{2,1,0:T(8,128)(2,1)} %get-tuple-element.10) | data formatting | bytes 262144
  103.4 1.6 %copy.11 = bf16[768,128]{1,0:T(8,128)(2,1)} copy(bf16[768,128]{1,0:T(8,128)(2,1)} %get-tuple-element.11) | data formatting | bytes 393216
  (2 shorter events, 0.0 us)
